TPU v7x, 32 devices: a whole 2x2x4 slice. The times are simulated.
32 devices in a mesh: dp: 4 (over z), expert: 8 (over y, x, core).
Axes of the slice: x: 2, y: 2, z: 4, core: 2. Of those that a mesh axis runs over, the one named last changes fastest.
Arguments:
- grad_parts: bfloat16 [4, 32, 128, 2048], P('dp', 'expert'), may hold values from -6 to 6
- first_moment: float32 [32, 128, 2048], P('expert', None, 'dp'), may hold values from -4 to 4
- second_moment: float32 [32, 128, 2048], P('expert', None, 'dp'), may hold values from 0.05 to 2
- master_weight: float32 [32, 128, 2048], P('expert', None, 'dp'), may hold values from -6 to 6
- old_owner: int32 [28], replicated, may hold values from 0 to 6, as said below
- new_owner: int32 [28], replicated, may hold values from 0 to 7, as said below
Outputs:
- new_master: float32 [48, 128, 2048], P('expert', None, 'dp')
- new_first: float32 [48, 128, 2048], P('expert', None, 'dp')
- new_second: float32 [48, 128, 2048], P('expert', None, 'dp')
- new_params: bfloat16 [48, 128, 2048], P('expert')
Inputs may be any that keep to these rules, and one draw needn't show every extreme that they name: `old_owner`: tiles are owned by devices 0 to 6 of the expert axis, exactly 4 each; the other devices own none, and their slots of the old-layout arrays are never read. `new_owner`: each device owns at most 6 tiles and some own exactly 6; the tiles of one old owner go to different new owners.
All inputs are finite; a program needn't handle non-finite values.
Results may differ from a plain program's by a relative error of at most 0.0085.
Values may be sent and summed in bfloat16 or wider, within the bound.
A program may use at most 128 MiB of HBM per device.

v0:
```python
import jax
import jax.numpy as jnp
from jax import lax
from jax.sharding import PartitionSpec as P


def slot_ranks(owner, count):
    matches = (owner[:, None] == jnp.arange(count, dtype=jnp.int32)[None, :]).astype(jnp.int32)
    before = jnp.cumsum(matches, axis=0) - matches
    return jnp.sum(before * matches, axis=1)


def adam_step(gradient, moment_one, moment_two, weight):
    moment_one = 0.9 * moment_one + 0.1 * gradient
    moment_two = 0.95 * moment_two + 0.05 * gradient * gradient
    update = moment_one / (1.0 - 0.9**50) / (jnp.sqrt(moment_two / (1.0 - 0.95**50)) + 1e-08)
    weight = weight - 0.05 * (update + 0.1 * weight)
    return (weight, moment_one, moment_two)


def shards(grad_parts, first_moment, second_moment, master_weight, old_owner, new_owner):
    peer_count = lax.axis_size("expert")
    device = lax.axis_index("expert")
    old_slots = first_moment.shape[0]
    new_slots = min(old_slots + old_slots // 2, peer_count - peer_count // 5)
    old_rank = slot_ranks(old_owner, peer_count)
    new_rank = slot_ranks(new_owner, peer_count)
    targets = jnp.arange(peer_count, dtype=jnp.int32)
    outgoing = (old_owner == device)[:, None] & (new_owner[:, None] == targets[None, :])
    send_has = jnp.sum(outgoing.astype(jnp.int32), axis=0) > 0
    send_slot = jnp.sum(jnp.where(outgoing, old_rank[:, None], 0), axis=0)
    slot_ids = jnp.arange(new_slots, dtype=jnp.int32)
    wanted = (new_owner == device)[:, None] & (new_rank[:, None] == slot_ids[None, :])
    recv_has = jnp.sum(wanted.astype(jnp.int32), axis=0) > 0
    recv_source = jnp.sum(jnp.where(wanted, old_owner[:, None], 0), axis=0)

    def to_peers(values):
        return jnp.where(send_has[:, None, None], values[send_slot], 0.0)

    def from_peers(values):
        return jnp.where(recv_has[:, None, None], values[recv_source], 0.0)

    summed = lax.psum_scatter(grad_parts[0], "dp", scatter_dimension=2, tiled=True).astype(
        jnp.float32
    )
    weight, moment_one, moment_two = adam_step(summed, first_moment, second_moment, master_weight)
    results = (
        lax.all_to_all(
            to_peers(weight).astype(jnp.bfloat16), "expert", split_axis=0, concat_axis=0, tiled=True
        ).astype(jnp.float32),
        lax.all_to_all(
            to_peers(moment_one).astype(jnp.bfloat16),
            "expert",
            split_axis=0,
            concat_axis=0,
            tiled=True,
        ).astype(jnp.float32),
        lax.all_to_all(
            to_peers(moment_two).astype(jnp.bfloat16),
            "expert",
            split_axis=0,
            concat_axis=0,
            tiled=True,
        ).astype(jnp.float32),
    )
    new_master = from_peers(results[0])
    new_first = from_peers(results[1])
    new_second = from_peers(results[2])
    new_params = lax.all_gather(new_master.astype(jnp.bfloat16), "dp", axis=2, tiled=True)
    return (new_master, new_first, new_second, new_params)


def solution(mesh):
    placed = (
        P("dp", "expert", None, None),
        P("expert", None, "dp"),
        P("expert", None, "dp"),
        P("expert", None, "dp"),
        P(),
        P(),
    )
    return jax.shard_map(
        shards,
        mesh=mesh,
        in_specs=placed,
        out_specs=(
            P("expert", None, "dp"),
            P("expert", None, "dp"),
            P("expert", None, "dp"),
            P("expert", None, None),
        ),
        check_vma=False,
    )
```

profile of v0, /device:TPU:0, one launch (start us, length us, event | category | flops | bytes accessed | tf_op | source)
XLA Modules:
  0.0 201.5 jit_solution(8720991101664355001)
XLA Ops:
  7.2 0.0 copy-start.3
  7.2 0.0 copy-start.2
  7.2 0.0 copy-start.1
  7.2 0.0 reduce-scatter.2.cloned.1.call-start
  7.2 0.7 reduce-scatter.2.cloned.1.call-update
  7.9 0.0 copy-done.3
  7.9 0.1 fusion.4
  8.0 0.1 reduce_window_sum.17
  8.1 0.0 copy-done.2
  8.1 0.1 fusion.2
  8.1 0.1 reduce_window_sum.18
  8.2 0.2 select_reduce_fusion.1
  8.4 0.2 convert_reduce_fusion
  8.6 48.1 %reduce-scatter.2.cloned.1.call-done = bf16[4,128,512]{2,1,0:T(8,128)(2,1)} async-done(((bf16[4,128,2048]{2,1,0:T(8,128)(2,1)}), bf16[4,128,512]{2,1,0:T(8,128)(2,1)}) %reduce-scatter.2.cloned.1.call-update) | async-done | bytes 524304 | tf_op jit(solution)/shard_map/reduce_scatter | solution.py:43
  56.7 0.0 copy-done.1
  56.7 2.6 %multiply_subtract_fusion = (bf16[4,128,512]{2,1,0:T(8,128)(2,1)S(1)}, bf16[4,128,512]{2,1,0:T(8,128)(2,1)S(1)}, bf16[4,128,512]{2,1,0:T(8,128)(2,1)S(1)}) fusion(f32[4,128,512]{2,1,0:T(8,128)S(1)} %copy-done.1, bf16[4,128,512]{2,1,0:T(8,128)(2,1)} %reduce-scatter.2.cloned.1.call-done, f32[4,128,512]{2,1,0:T(8,128)} %param.7, f32[4,128,512]{2,1,0:T(8,128)} %param.8), kind=kLoop, calls=%fused_computation.13 | loop fusion | flops 4980736 | bytes 5242880 | tf_op jit(solution)/shard_map/sub | solution.py:17
  59.3 0.6 gather_fusion
  59.9 1.6 gather_fusion.2
  61.5 0.0 copy-start
  61.5 1.6 gather_fusion.4
  63.1 0.0 copy-done
  63.1 3.1 %select_convert_fusion = (bf16[8,128,512]{2,1,0:T(8,128)(2,1)}, bf16[8,128,512]{2,1,0:T(8,128)(2,1)S(1)}, bf16[8,128,512]{2,1,0:T(8,128)(2,1)S(1)}) fusion(bf16[8,128,512]{2,1,0:T(8,128)(2,1)} %gather_fusion.4, pred[8]{0:T(512)(128)(4,1)S(1)} %broadcast_compare_fusion, bf16[8,128,512]{2,1,0:T(8,128)(2,1)S(1)} %copy-done, bf16[8,128,512]{2,1,0:T(8,128)(2,1)S(1)} %gather_fusion), kind=kLoop, calls=%fused_computation.6 | loop fusion | flops 1572864 | bytes 6291464 | tf_op jit(solution)/shard_map/convert_element_type | solution.py:59
  66.2 18.9 %all_to_all.15 = bf16[8,128,512]{2,1,0:T(8,128)(2,1)} all-to-all(bf16[8,128,512]{2,1,0:T(8,128)(2,1)S(1)} %get-tuple-element.19), channel_id=1, replica_groups=mesh['dp'=4,'expert'=8] {'expert'}, dimensions={0} | all-to-all | bytes 2097152 | tf_op jit(solution)/shard_map/all_to_all | solution.py:51
  85.1 18.4 %all_to_all.16 = bf16[8,128,512]{2,1,0:T(8,128)(2,1)} all-to-all(bf16[8,128,512]{2,1,0:T(8,128)(2,1)S(1)} %get-tuple-element.20), channel_id=1, replica_groups=mesh['dp'=4,'expert'=8] {'expert'}, dimensions={0} | all-to-all | bytes 2097152 | tf_op jit(solution)/shard_map/all_to_all | solution.py:48
  103.5 3.6 %all-to-all-start.2 = ((bf16[8,128,512]{2,1,0:T(8,128)(2,1)}), bf16[8,128,512]{2,1,0:T(8,128)(2,1)S(1)}, u32[]{:S(2)}, u32[]{:S(2)}) async-start(bf16[8,128,512]{2,1,0:T(8,128)(2,1)} %get-tuple-element.18), calls=%async_computation.3 | async-start | bytes 2097152 | tf_op jit(solution)/shard_map/all_to_all | solution.py:58
  107.1 0.0 all-gather.2.cloned.1.call-start
  107.2 0.1 convert_reduce_fusion.1
  107.3 1.5 convert_element_type.42
  108.9 1.8 gather_fusion.1
  110.7 1.5 convert_element_type.44
  112.2 1.8 gather_fusion.3
  114.0 8.5 %all-to-all-done.2 = bf16[8,128,512]{2,1,0:T(8,128)(2,1)S(1)} async-done(((bf16[8,128,512]{2,1,0:T(8,128)(2,1)}), bf16[8,128,512]{2,1,0:T(8,128)(2,1)S(1)}, u32[]{:S(2)}, u32[]{:S(2)}) %all-to-all-start.2) | async-done | bytes 1048608 | tf_op jit(solution)/shard_map/all_to_all | solution.py:58
  122.4 0.3 convert_element_type.46
  122.7 1.8 gather_fusion.5
  124.5 5.1 %broadcast_select_fusion = (f32[6,128,512]{2,1,0:T(8,128)}, f32[6,128,512]{2,1,0:T(8,128)}, bf16[6,128,512]{2,1,0:T(8,128)(2,1)}, f32[6,128,512]{2,1,0:T(8,128)}) fusion(f32[6,128,512]{2,1,0:T(8,128)} %gather_fusion.5, pred[6]{0:T(512)(128)(4,1)S(1)} %broadcast_compare_fusion.1, f32[6,128,512]{2,1,0:T(8,128)} %gather_fusion.3, f32[6,128,512]{2,1,0:T(8,128)} %gather_fusion.1), kind=kLoop, calls=%fused_computation.14 | loop fusion | flops 1572864 | bytes 10223622 | tf_op jit(solution)/shard_map/jit(_where)/select_n | solution.py:41
  129.6 0.0 all-gather.2.cloned.1.call-update
  129.6 61.0 %all-gather.2.cloned.1.call-done = bf16[6,128,2048]{2,1,0:T(8,128)(2,1)} async-done(((bf16[6,128,512]{2,1,0:T(8,128)(2,1)}), bf16[6,128,2048]{2,1,0:T(8,128)(2,1)}) %all-gather.2.cloned.1.call-update) | async-done | bytes 3145744 | tf_op jit(solution)/shard_map/all_gather | solution.py:69
  190.6 4.0 %copy.11 = bf16[6,128,2048]{2,1,0:T(8,128)(2,1)} copy(bf16[6,128,2048]{2,1,0:T(8,128)(2,1)} %all-gather.2.cloned.1.call-done) | data formatting | bytes 6291456
  (7 shorter events, 0.0 us)
Async XLA Ops:
  7.2 0.8 copy-start.3
  7.2 0.9 copy-start.2
  7.2 49.5 %copy-start.1 = (f32[4,128,512]{2,1,0:T(8,128)S(1)}, f32[4,128,512]{2,1,0:T(8,128)}, u32[]{:S(2)}) copy-start(f32[4,128,512]{2,1,0:T(8,128)} %param.9) | copy-start | bytes 3145732
  7.2 49.5 %reduce-scatter.2.cloned.1.call-start = ((), (), s32[]{:S(2)}) async-start(), calls=%async_computation.4 | async-start | bytes 2621440 | tf_op jit(solution)/shard_map/reduce_scatter | solution.py:43
  61.5 1.6 copy-start
  103.5 18.9 %all-to-all-start.2 = ((bf16[8,128,512]{2,1,0:T(8,128)(2,1)}), bf16[8,128,512]{2,1,0:T(8,128)(2,1)S(1)}, u32[]{:S(2)}, u32[]{:S(2)}) async-start(bf16[8,128,512]{2,1,0:T(8,128)(2,1)} %get-tuple-element.18), calls=%async_computation.3 | async-start | bytes 2097152 | tf_op jit(solution)/shard_map/all_to_all | solution.py:58
  107.1 83.5 %all-gather.2.cloned.1.call-start = ((), (), s32[]{:S(2)}) async-start(), calls=%async_computation.5 | async-start | bytes 3932160 | tf_op jit(solution)/shard_map/all_gather | solution.py:69
Sparse Core Ops, SparseCore 0:
  10.3 46.3 reduce-scatter.1
  129.7 60.8 all-gather.1
where the time goes:
time: 202 us; the launch traced here: 201 us
  waiting for transfers between devices  118 us (58%)
  blocking collectives  37.3 us (18%)
  other arithmetic  14.9 us (7%)
  between operations  14.2 us (7%)
  local copies, waits for them, and re-layouts  13.1 us (6%)
  starting transfers between devices  3.64 us (2%)
    all_gather x1, waiting for transfers between devices, shards(): lax.all_gather(new_master.astype(jnp.bfloat16), 'dp', axis=2, tiled=True)  61 us
    reduce_scatter x1, waiting for transfers between devices, shards(): lax.psum_scatter(grad_parts[0], 'dp', scatter_dimension=2, tiled=True)  48.1 us
    all_to_all x1, blocking collectives, shards(): lax.all_to_all(to_peers(moment_one).astype(jnp.bfloat16), 'expert', split...  18.9 us
    all_to_all x1, blocking collectives, shards(): lax.all_to_all(to_peers(weight).astype(jnp.bfloat16), 'expert', split_axi...  18.4 us
    all_to_all x1, waiting for transfers between devices, shards(): lax.all_to_all(to_peers(moment_two).astype(jnp.bfloat16), 'expert', split...  8.47 us
    gather x3, local copies, waits for them, and re-layouts, from_peers(): return jnp.where(recv_has[:, None, None], values[recv_source], 0.0)  5.39 us
    select_n x2, other arithmetic, from_peers(): return jnp.where(recv_has[:, None, None], values[recv_source], 0.0)  5.1 us
  transfers between devices with their start and end apart: 3, of which 3 were waited for; matrix products, arithmetic and copies ran while one was open for 4% of the time, Pallas kernels for 0%

commit v1 on v0

v1 whole, which is shorter than its diff:
```python
import functools

import jax
import jax.numpy as jnp
from jax import lax
from jax.experimental import pallas as pl
from jax.experimental.pallas import tpu as pltpu
from jax.sharding import PartitionSpec as P

MESH = pl.DeviceIdType.MESH
ROWS = 32
AHEAD = 1


def slot_ranks(owner):
    earlier = jnp.tril(jnp.ones((owner.shape[0],) * 2, jnp.bool_), -1)
    return jnp.sum(((owner[:, None] == owner[None, :]) & earlier).astype(jnp.int32), axis=1)


def adam_step(gradient, moment_one, moment_two, weight):
    moment_one = 0.9 * moment_one + 0.1 * gradient
    moment_two = 0.95 * moment_two + 0.05 * gradient * gradient
    update = moment_one / (1.0 - 0.9**50) / (jnp.sqrt(moment_two / (1.0 - 0.95**50)) + 1e-08)
    weight = weight - 0.05 * (update + 0.1 * weight)
    return (weight, moment_one, moment_two)


def kernel(dp, peers, owners, chunks, slot_ref, source_ref, has_ref, g_hbm, m_hbm, v_hbm, w_hbm, *rest):
    outs, params_out, rest = rest[:3], rest[3], rest[4:]
    g, state, part, up, down, stay, params = rest[:7]
    rest = rest[7:]
    fresh, mail, inbox, final = (rest[i * chunks : (i + 1) * chunks] for i in range(4))
    (in_sem, up_send, up_recv, down_send, down_recv, x_send, x_recv,
     gu_send, gu_recv, gd_send, gd_recv, out_sem, params_sem) = rest[4 * chunks :]
    z = lax.axis_index("dp")
    e = lax.axis_index("expert")
    cols = stay.shape[-1]
    new_slots = params.shape[0]
    mine = pl.ds(pl.multiple_of(z * cols, cols), cols)
    owns = e < owners

    loads = [pltpu.make_async_copy(g_hbm.at[0], g, in_sem.at[0])]
    loads += [
        pltpu.make_async_copy(ref, state.at[i], in_sem.at[i + 1])
        for i, ref in enumerate((m_hbm, v_hbm, w_hbm))
    ]
    for load in loads:
        load.start()

    barrier = pltpu.get_barrier_semaphore()
    for step in range(1, peers):
        pl.semaphore_signal(
            barrier, inc=1, device_id={"expert": lax.rem(e + step, peers)}, device_id_type=MESH
        )

    @pl.when(z > 0)
    def _():
        pl.semaphore_signal(barrier, inc=1, device_id={"dp": z - 1}, device_id_type=MESH)

    @pl.when(z < dp - 1)
    def _():
        pl.semaphore_signal(barrier, inc=1, device_id={"dp": z + 1}, device_id_type=MESH)

    inner = (z > 0).astype(jnp.int32) + (z < dp - 1).astype(jnp.int32)
    pl.semaphore_wait(barrier, peers - 1 + inner)
    for load in loads:
        load.wait()

    def rows(c):
        return pl.ds(c * ROWS, ROWS)

    def block(k):
        return pl.ds(k * cols, cols)

    def up_copy(c, k, raw):
        src = g.at[:, rows(c), block(k)] if raw else part.at[k, :, rows(c)]
        return pltpu.make_async_remote_copy(
            src, up.at[k, :, rows(c)], up_send.at[c, k], up_recv.at[c, k],
            device_id={"dp": z + 1}, device_id_type=MESH,
        )

    def down_copy(c, k, raw):
        src = g.at[:, rows(c), block(k)] if raw else part.at[k, :, rows(c)]
        return pltpu.make_async_remote_copy(
            src, down.at[k, :, rows(c)], down_send.at[c, k], down_recv.at[c, k],
            device_id={"dp": z - 1}, device_id_type=MESH,
        )

    def gather_copy(c, k, going_up):
        send, recv = (gu_send, gu_recv) if going_up else (gd_send, gd_recv)
        where = params.at[:, rows(c), block(k)]
        return pltpu.make_async_remote_copy(
            where, where, send.at[c, k], recv.at[c, k],
            device_id={"dp": z + 1 if going_up else z - 1}, device_id_type=MESH,
        )

    def mail_copy(c, to, source):
        return pltpu.make_async_remote_copy(
            mail[c].at[to], inbox[c].at[source], x_send.at[c, to], x_recv.at[c, source],
            device_id={"expert": to}, device_id_type=MESH,
        )

    def first_sends(c):
        @pl.when(owns & (z == 0))
        def _():
            for k in range(dp - 1, 0, -1):
                up_copy(c, k, True).start()

        @pl.when(owns & (z == dp - 1))
        def _():
            for k in range(dp - 1):
                down_copy(c, k, True).start()

    def relay_up(c):
        for k in range(dp - 1, 0, -1):
            @pl.when(owns & (z > 0) & (z < k))
            def _():
                up_copy(c, k, False).wait_recv()
                total = g[:, rows(c), block(k)].astype(jnp.float32) + up[k, :, rows(c)].astype(jnp.float32)
                part[k, :, rows(c)] = total.astype(jnp.bfloat16)
                up_copy(c, k, False).start()

    def relay_down(c):
        for k in range(dp - 1):
            @pl.when(owns & (z < dp - 1) & (z > k))
            def _():
                down_copy(c, k, False).wait_recv()
                total = g[:, rows(c), block(k)].astype(jnp.float32) + down[k, :, rows(c)].astype(jnp.float32)
                part[k, :, rows(c)] = total.astype(jnp.bfloat16)
                down_copy(c, k, False).start()

    def ordered(first, second):
        @pl.when(z * 2 < dp)
        def _():
            first()
            second()

        @pl.when(z * 2 >= dp)
        def _():
            second()
            first()

    def update(c):
        @pl.when(owns)
        def _():
            stay[:, rows(c)] = g[:, rows(c), mine].astype(jnp.float32)
            for k in range(dp):
                @pl.when(z == k)
                def _():
                    if k > 0:
                        up_copy(c, k, False).wait_recv()
                        stay[:, rows(c)] += up[k, :, rows(c)].astype(jnp.float32)
                    if k < dp - 1:
                        down_copy(c, k, False).wait_recv()
                        stay[:, rows(c)] += down[k, :, rows(c)].astype(jnp.float32)
            for slot in range(stay.shape[0]):
                values = adam_step(
                    stay[slot, rows(c)], state[0, slot, rows(c)], state[1, slot, rows(c)], state[2, slot, rows(c)]
                )
                for i, value in enumerate(values):
                    fresh[c][slot, i] = value.astype(jnp.bfloat16)
            for step in range(1, peers):
                to = lax.rem(e + step, peers)
                mail[c][to] = fresh[c][slot_ref[to]]
                mail_copy(c, to, e).start()
            inbox[c][e] = fresh[c][slot_ref[e]]

    def deliver(c):
        for source in range(owners):
            @pl.when(e != source)
            def _():
                mail_copy(c, source, source).wait_recv()
        for slot in range(new_slots):
            present = has_ref[slot] > 0
            for i in range(3):
                value = inbox[c][source_ref[slot], i]
                value = jnp.where(present, value, jnp.zeros_like(value))
                final[c][i, slot] = value.astype(jnp.float32)
                if i == 0:
                    params[slot, rows(c), mine] = value
        for i in range(3):
            pltpu.make_async_copy(final[c].at[i], outs[i].at[:, rows(c)], out_sem.at[c, i]).start()
        for k in range(dp):
            @pl.when(z == k)
            def _():
                if k < dp - 1:
                    gather_copy(c, k, True).start()
                if k > 0:
                    gather_copy(c, k, False).start()

    def spread(c):
        def upward():
            for k in range(dp - 2, -1, -1):
                @pl.when(z > k)
                def _():
                    gather_copy(c, k, True).wait_recv()

                    @pl.when(z < dp - 1)
                    def _():
                        gather_copy(c, k, True).start()

        def downward():
            for k in range(1, dp):
                @pl.when(z < k)
                def _():
                    gather_copy(c, k, False).wait_recv()

                    @pl.when(z > 0)
                    def _():
                        gather_copy(c, k, False).start()

        ordered(upward, downward)
        pltpu.make_async_copy(params.at[:, rows(c)], params_out.at[:, rows(c)], params_sem.at[c]).start()

    for c in range(min(AHEAD, chunks)):
        first_sends(c)
    for c in range(chunks + 2):
        if c < chunks:
            if c + AHEAD < chunks:
                first_sends(c + AHEAD)
            ordered(functools.partial(relay_up, c), functools.partial(relay_down, c))
            update(c)
        if 1 <= c <= chunks:
            deliver(c - 1)
        if c >= 2:
            spread(c - 2)

    for c in range(chunks):
        @pl.when(owns)
        def _():
            for k in range(1, dp):
                @pl.when(z < k)
                def _():
                    up_copy(c, k, False).wait_send()
            for k in range(dp - 1):
                @pl.when(z > k)
                def _():
                    down_copy(c, k, False).wait_send()
            for step in range(1, peers):
                mail_copy(c, lax.rem(e + step, peers), e).wait_send()
        for k in range(dp):
            @pl.when((z >= k) & (z < dp - 1))
            def _():
                gather_copy(c, k, True).wait_send()

            @pl.when((z <= k) & (z > 0))
            def _():
                gather_copy(c, k, False).wait_send()
        for i in range(3):
            pltpu.make_async_copy(final[c].at[i], outs[i].at[:, rows(c)], out_sem.at[c, i]).wait()
        pltpu.make_async_copy(params.at[:, rows(c)], params_out.at[:, rows(c)], params_sem.at[c]).wait()


def shards(grad_parts, first_moment, second_moment, master_weight, old_owner, new_owner):
    dp = lax.axis_size("dp")
    peers = lax.axis_size("expert")
    device = lax.axis_index("expert")
    old_slots, tile_rows, cols = first_moment.shape
    owners = old_owner.shape[0] // old_slots
    new_slots = min(old_slots + old_slots // 2, peers - peers // 5)
    chunks = tile_rows // ROWS
    old_rank = slot_ranks(old_owner)
    new_rank = slot_ranks(new_owner)
    targets = jnp.arange(peers, dtype=jnp.int32)
    outgoing = (old_owner == device)[None, :] & (new_owner[None, :] == targets[:, None])
    send_slot = jnp.sum(jnp.where(outgoing, old_rank[None, :], 0), axis=1)
    slot_ids = jnp.arange(new_slots, dtype=jnp.int32)
    wanted = (new_owner == device)[None, :] & (new_rank[None, :] == slot_ids[:, None])
    recv_has = jnp.sum(wanted.astype(jnp.int32), axis=1)
    recv_source = jnp.sum(jnp.where(wanted, old_owner[None, :], 0), axis=1)

    bf16, f32 = jnp.bfloat16, jnp.float32
    dma = pltpu.SemaphoreType.DMA
    any_space = pl.BlockSpec(memory_space=pl.ANY)
    smem = pl.BlockSpec(memory_space=pltpu.SMEM)
    master = jax.ShapeDtypeStruct((new_slots, tile_rows, cols), f32)
    scratch = [
        pltpu.VMEM((old_slots, tile_rows, dp * cols), bf16),
        pltpu.VMEM((3, old_slots, tile_rows, cols), f32),
        pltpu.VMEM((dp, old_slots, tile_rows, cols), bf16),
        pltpu.VMEM((dp, old_slots, tile_rows, cols), bf16),
        pltpu.VMEM((dp, old_slots, tile_rows, cols), bf16),
        pltpu.VMEM((old_slots, tile_rows, cols), f32),
        pltpu.VMEM((new_slots, tile_rows, dp * cols), bf16),
    ]
    scratch += [pltpu.VMEM((old_slots, 3, ROWS, cols), bf16)] * chunks
    scratch += [pltpu.VMEM((peers, 3, ROWS, cols), bf16)] * chunks
    scratch += [pltpu.VMEM((peers, 3, ROWS, cols), bf16)] * chunks
    scratch += [pltpu.VMEM((3, new_slots, ROWS, cols), f32)] * chunks
    scratch += [dma((4,))] + [dma((chunks, dp))] * 4 + [dma((chunks, peers))] * 2
    scratch += [dma((chunks, dp))] * 4 + [dma((chunks, 3)), dma((chunks,))]
    return pl.pallas_call(
        functools.partial(kernel, dp, peers, owners, chunks),
        out_shape=(master,) * 3
        + (jax.ShapeDtypeStruct((new_slots, tile_rows, dp * cols), bf16),),
        in_specs=[smem] * 3 + [any_space] * 4,
        out_specs=(any_space,) * 4,
        scratch_shapes=scratch,
        compiler_params=pltpu.CompilerParams(
            collective_id=0, has_side_effects=True, vmem_limit_bytes=60 * 2**20
        ),
    )(send_slot, recv_source, recv_has, grad_parts, first_moment, second_moment, master_weight)


def solution(mesh):
    placed = (
        P("dp", "expert", None, None),
        P("expert", None, "dp"),
        P("expert", None, "dp"),
        P("expert", None, "dp"),
        P(),
        P(),
    )
    return jax.shard_map(
        shards,
        mesh=mesh,
        in_specs=placed,
        out_specs=(
            P("expert", None, "dp"),
            P("expert", None, "dp"),
            P("expert", None, "dp"),
            P("expert", None, None),
        ),
        check_vma=False,
    )
```

time: 202 us -> 111 us (0.55)
  waiting for transfers between devices: 118 us -> 0 us
  Pallas kernels: 0 us -> 97.2 us
  blocking collectives: 37.3 us -> 0 us
  between operations: 14.2 us -> 0.66 us
  other arithmetic: 14.9 us -> 4.21 us
  local copies, waits for them, and re-layouts: 13.1 us -> 8.98 us
  starting transfers between devices: 3.64 us -> 0 us
    pallas_call x0 -> x1, Pallas kernels: none -> 97.2 us  [shards(): pl.pallas_call(functools.partial(kernel, dp, peers, owners, chunks), out_...]
    all_gather x1 -> x0, waiting for transfers between devices: 61 us -> none  [shards(): lax.all_gather(new_master.astype(jnp.bfloat16), 'dp', axis=2, tiled=True)]
    reduce_scatter x1 -> x0, waiting for transfers between devices: 48.1 us -> none  [shards(): lax.psum_scatter(grad_parts[0], 'dp', scatter_dimension=2, tiled=True)]
    all_to_all x2 -> x0, blocking collectives: 37.3 us -> none  [the longest x1 18.9 us: shards(): lax.all_to_all(to_peers(moment_one).astype(jnp.bfloat16), 'expert', split...]
    gather x6 -> x0, local copies, waits for them, and re-layouts: 9.16 us -> none  [the longest x3 5.39 us: from_peers(): return jnp.where(recv_has[:, None, None], values[recv_source], 0.0)]
    all_to_all x1 -> x0, waiting for transfers between devices: 8.47 us -> none  [shards(): lax.all_to_all(to_peers(moment_two).astype(jnp.bfloat16), 'expert', split...]
    convert_element_type x6 -> x0, other arithmetic: 6.53 us -> none  [the longest x3 3.27 us: shards(): results = (lax.all_to_all(to_peers(weight).astype(jnp.bfloat16), 'expert'...]
    select_n x3 -> x0, other arithmetic: 5.11 us -> none  [the longest x2 5.1 us: from_peers(): return jnp.where(recv_has[:, None, None], values[recv_source], 0.0)]
  transfers between devices with their start and end apart: 3 -> 0, of which waited for: 3 -> 0; matrix products, arithmetic and copies ran while one was open for 4% -> 0% of each run, Pallas kernels for 0% -> 0%
where the time goes in v1:
time: 111 us
  Pallas kernels  97.2 us (88%)
  local copies, waits for them, and re-layouts  8.98 us (8%)
  other arithmetic  4.21 us (4%)
    pallas_call x1, Pallas kernels, shards(): pl.pallas_call(functools.partial(kernel, dp, peers, owners, chunks), out_...  97.2 us
    unnamed x10, local copies, waits for them, and re-layouts  8.98 us

profile of v1, /device:TPU:0, one launch (start us, length us, event | category | flops | bytes accessed | tf_op | source)
XLA Modules:
  0.0 111.0 jit_solution(16517140916967145238)
XLA Ops:
  0.6 0.9 convert_reduce_fusion
  1.6 0.7 broadcast_compare_fusion
  2.3 1.3 %select_reduce_fusion.1.slot_ref = s32[8]{0:T(128)} fusion(s32[28]{0:T(128)S(1)} %get-tuple-element.7, s32[28]{0:T(128)} %param.11, pred[28]{0:T(512)(128)(4,1)S(1)} %get-tuple-element.9), kind=kLoop, calls=%fused_computation.8 | loop fusion | flops 888 | bytes 284 | tf_op jit(solution)/shard_map/reduce_sum | solution.py:266
  3.5 1.3 %convert_reduce_fusion.2 = (s32[6]{0:T(128)}, s32[6]{0:T(128)}) fusion(s32[28]{0:T(128)S(1)} %get-tuple-element.6, pred[28]{0:T(512)(128)(4,1)S(1)} %get-tuple-element.8, s32[28]{0:T(128)} %param.10), kind=kLoop, calls=%fused_computation.5 | loop fusion | flops 996 | bytes 300 | tf_op jit(solution)/shard_map/reduce_sum | solution.py:269
  4.9 97.2 %shard_map.93 = (f32[6,128,512]{2,1,0:T(8,128)}, f32[6,128,512]{2,1,0:T(8,128)}, f32[6,128,512]{2,1,0:T(8,128)}, bf16[6,128,2048]{2,1,0:T(8,128)(2,1)}) custom-call(s32[8]{0:T(128)} %select_reduce_fusion.1.slot_ref, s32[6]{0:T(128)} %get-tuple-element.5.source_ref, s32[6]{0:T(128)} %get-tuple-element.4.has_ref, bf16[1,4,128,2048]{3,2,1,0:T(8,128)(2,1)} %g_hbm.1, ...), custom_call_target="tpu_custom_call" | custom-call | tf_op jit(solution)/shard_map/pallas_call | solution.py:292
  102.0 0.0 copy-start.2
  102.1 2.9 %copy.14 = f32[6,128,512]{2,1,0:T(8,128)} copy(f32[6,128,512]{2,1,0:T(8,128)} %get-tuple-element.14) | data formatting | bytes 3145728
  104.9 0.0 copy-done.2
  104.9 0.0 copy-start.1
  104.9 1.1 %copy.15 = f32[6,128,512]{2,1,0:T(8,128)} copy(f32[6,128,512]{2,1,0:T(8,128)S(1)} %copy-done.2) | data formatting | bytes 3145728
  106.1 0.8 copy-done.1
  106.9 0.0 copy-start
  106.9 1.1 %copy.16 = f32[6,128,512]{2,1,0:T(8,128)} copy(f32[6,128,512]{2,1,0:T(8,128)S(1)} %copy-done.1) | data formatting | bytes 3145728
  108.1 1.3 %copy-done = bf16[6,128,2048]{2,1,0:T(8,128)(2,1)S(1)} copy-done((bf16[6,128,2048]{2,1,0:T(8,128)(2,1)S(1)}, bf16[6,128,2048]{2,1,0:T(8,128)(2,1)}, u32[]{:S(2)}) %copy-start) | copy-done | bytes 3145752
  109.4 1.7 %copy.17 = bf16[6,128,2048]{2,1,0:T(8,128)(2,1)} copy(bf16[6,128,2048]{2,1,0:T(8,128)(2,1)S(1)} %copy-done) | data formatting | bytes 6291456
  (1 shorter events, 0.0 us)
Async XLA Ops:
  102.0 2.9 %copy-start.2 = (f32[6,128,512]{2,1,0:T(8,128)S(1)}, f32[6,128,512]{2,1,0:T(8,128)}, u32[]{:S(2)}) copy-start(f32[6,128,512]{2,1,0:T(8,128)} %get-tuple-element.15) | copy-start | bytes 4718596
  104.9 2.0 %copy-start.1 = (f32[6,128,512]{2,1,0:T(8,128)S(1)}, f32[6,128,512]{2,1,0:T(8,128)}, u32[]{:S(2)}) copy-start(f32[6,128,512]{2,1,0:T(8,128)} %get-tuple-element.16) | copy-start | bytes 4718596
  106.9 2.5 %copy-start = (bf16[6,128,2048]{2,1,0:T(8,128)(2,1)S(1)}, bf16[6,128,2048]{2,1,0:T(8,128)(2,1)}, u32[]{:S(2)}) copy-start(bf16[6,128,2048]{2,1,0:T(8,128)(2,1)} %get-tuple-element.17) | copy-start | bytes 9437188

commit v2 on v1

v2 whole, which is shorter than its diff:
```python
import functools

import jax
import jax.numpy as jnp
from jax import lax
from jax.experimental import pallas as pl
from jax.experimental.pallas import tpu as pltpu
from jax.sharding import PartitionSpec as P

MESH = pl.DeviceIdType.MESH
ROWS = 16
AHEAD = 1
HOP = 1
MAIL = 2
WIDE = 2
PLAN = (1, 0)


def early(c):
    return PLAN[c % len(PLAN)] == 1


def adam_step(gradient, moment_one, moment_two, weight):
    moment_one = 0.9 * moment_one + 0.1 * gradient
    moment_two = 0.95 * moment_two + 0.05 * gradient * gradient
    update = moment_one / (1.0 - 0.9**50) / (jnp.sqrt(moment_two / (1.0 - 0.95**50)) + 1e-08)
    weight = weight - 0.05 * (update + 0.1 * weight)
    return (weight, moment_one, moment_two)


def kernel(dp, peers, owners, chunks, old_ref, new_ref, g_hbm, m_hbm, v_hbm, w_hbm, *rest):
    outs, params, rest = rest[:3], rest[3], rest[4:]
    g, state, part, up, down, stay = rest[:6]
    rest = rest[6:]
    fresh, mail, inbox, wide, wide_mail, wide_inbox = (rest[i * chunks : (i + 1) * chunks] for i in range(6))
    (in_sem, up_send, up_recv, down_send, down_recv, x_send, x_recv, w_send, w_recv,
     gu_send, gu_recv, gd_send, gd_recv) = rest[6 * chunks :]
    z = lax.axis_index("dp")
    e = lax.axis_index("expert")
    cols = stay.shape[-1]
    new_slots = params.shape[0]
    mine = pl.ds(pl.multiple_of(z * cols, cols), cols)
    owns = e < owners

    loads = [pltpu.make_async_copy(g_hbm.at[0], g, in_sem.at[0])]
    loads += [
        pltpu.make_async_copy(ref, state.at[i], in_sem.at[i + 1])
        for i, ref in enumerate((m_hbm, v_hbm, w_hbm))
    ]
    for load in loads:
        load.start()

    barrier = pltpu.get_barrier_semaphore()
    for step in range(1, peers):
        pl.semaphore_signal(
            barrier, inc=1, device_id={"expert": lax.rem(e + step, peers)}, device_id_type=MESH
        )

    @pl.when(z > 0)
    def _():
        pl.semaphore_signal(barrier, inc=1, device_id={"dp": z - 1}, device_id_type=MESH)

    @pl.when(z < dp - 1)
    def _():
        pl.semaphore_signal(barrier, inc=1, device_id={"dp": z + 1}, device_id_type=MESH)

    inner = (z > 0).astype(jnp.int32) + (z < dp - 1).astype(jnp.int32)
    pl.semaphore_wait(barrier, peers - 1 + inner)
    for load in loads:
        load.wait()

    tiles = old_ref.shape[0]
    targets = [lax.rem(e + step, peers) for step in range(peers)]

    def route(tile, carry):
        sent, taken, slots, sources = carry
        old, new = old_ref[tile], new_ref[tile]
        leaves, comes = old == e, new == e
        slots = tuple(jnp.where(leaves & (new == to), sent, slot) for to, slot in zip(targets, slots))
        sources = tuple(
            jnp.where(comes & (taken == slot), old, source) for slot, source in enumerate(sources)
        )
        return sent + leaves.astype(jnp.int32), taken + comes.astype(jnp.int32), slots, sources

    def rows(c):
        return pl.ds(c * ROWS, ROWS)

    def block(k):
        return pl.ds(k * cols, cols)

    def up_copy(c, k, raw):
        src = g.at[:, rows(c), block(k)] if raw else part.at[k, :, rows(c)]
        return pltpu.make_async_remote_copy(
            src, up.at[k, :, rows(c)], up_send.at[c, k], up_recv.at[c, k],
            device_id={"dp": z + 1}, device_id_type=MESH,
        )

    def down_copy(c, k, raw):
        src = g.at[:, rows(c), block(k)] if raw else part.at[k, :, rows(c)]
        return pltpu.make_async_remote_copy(
            src, down.at[k, :, rows(c)], down_send.at[c, k], down_recv.at[c, k],
            device_id={"dp": z - 1}, device_id_type=MESH,
        )

    def gather_copy(c, k, going_up):
        send, recv = (gu_send, gu_recv) if going_up else (gd_send, gd_recv)
        where = wide[c].at[:, :, block(k)] if early(c) else params.at[:, rows(c), block(k)]
        return pltpu.make_async_remote_copy(
            where, where, send.at[c, k], recv.at[c, k],
            device_id={"dp": z + 1 if going_up else z - 1}, device_id_type=MESH,
        )

    def mail_copy(c, to, source):
        return pltpu.make_async_remote_copy(
            mail[c].at[to], inbox[c].at[source], x_send.at[c, to], x_recv.at[c, source],
            device_id={"expert": to}, device_id_type=MESH,
        )

    def wide_copy(c, to, source):
        return pltpu.make_async_remote_copy(
            wide_mail[c].at[to], wide_inbox[c].at[source], w_send.at[c, to], w_recv.at[c, source],
            device_id={"expert": to}, device_id_type=MESH,
        )

    def first_sends(c):
        @pl.when(owns & (z == 0))
        def _():
            for k in range(dp - 1, 0, -1):
                up_copy(c, k, True).start()

        @pl.when(owns & (z == dp - 1))
        def _():
            for k in range(dp - 1):
                down_copy(c, k, True).start()

    def relay_up(c, at):
        for k in range(dp - 1, at, -1):
            up_copy(c, k, False).wait_recv()
            total = g[:, rows(c), block(k)].astype(jnp.float32) + up[k, :, rows(c)].astype(jnp.float32)
            part[k, :, rows(c)] = total.astype(jnp.bfloat16)
            up_copy(c, k, False).start()

    def relay_down(c, at):
        for k in range(at):
            down_copy(c, k, False).wait_recv()
            total = g[:, rows(c), block(k)].astype(jnp.float32) + down[k, :, rows(c)].astype(jnp.float32)
            part[k, :, rows(c)] = total.astype(jnp.bfloat16)
            down_copy(c, k, False).start()

    def relay(c, at, going_up):
        @pl.when(owns & (z == at))
        def _():
            (relay_up if going_up else relay_down)(c, at)

    def update(c):
        @pl.when(owns)
        def _():
            stay[...] = g[:, rows(c), mine].astype(jnp.float32)
            for k in range(dp):
                @pl.when(z == k)
                def _():
                    if k > 0:
                        up_copy(c, k, False).wait_recv()
                        stay[...] += up[k, :, rows(c)].astype(jnp.float32)
                    if k < dp - 1:
                        down_copy(c, k, False).wait_recv()
                        stay[...] += down[k, :, rows(c)].astype(jnp.float32)
            for slot in range(stay.shape[0]):
                values = adam_step(
                    stay[slot], state[0, slot, rows(c)], state[1, slot, rows(c)], state[2, slot, rows(c)]
                )
                values = [value.astype(jnp.bfloat16) for value in values]
                if early(c):
                    wide[c][slot, :, mine] = values.pop(0)
                for i, value in enumerate(values):
                    fresh[c][slot, i] = value
            if early(c):
                gather(c)
            for to, slot in zip(targets[1:], slots[1:]):
                mail[c][to] = fresh[c][slot]
                mail_copy(c, to, e).start()
            inbox[c][e] = fresh[c][slots[0]]

    def gather(c):
        for k in range(dp):
            @pl.when(z == k)
            def _():
                if k < dp - 1:
                    gather_copy(c, k, True).start()
                if k > 0:
                    gather_copy(c, k, False).start()

    def forward(c, hop):
        for at in range(1, dp - 1):
            @pl.when((owns & (z == at)) if early(c) else (z == at))
            def _():
                for k, going_up in ((at - hop, True), (at + hop, False)):
                    if 0 <= k < dp:
                        gather_copy(c, k, going_up).wait_recv()
                        gather_copy(c, k, going_up).start()

    def gathered(c):
        @pl.when(z == dp - 1)
        def _():
            for k in range(dp - 1):
                gather_copy(c, k, True).wait_recv()

        @pl.when(z == 0)
        def _():
            for k in range(1, dp):
                gather_copy(c, k, False).wait_recv()

    def post_wide(c):
        @pl.when(owns)
        def _():
            gathered(c)
            for to, slot in zip(targets[1:], slots[1:]):
                wide_mail[c][to] = wide[c][slot]
                wide_copy(c, to, e).start()
            wide_inbox[c][e] = wide[c][slots[0]]

    def deliver(c):
        for source in range(owners):
            @pl.when(e != source)
            def _():
                mail_copy(c, source, source).wait_recv()
                if early(c):
                    wide_copy(c, source, source).wait_recv()

        for slot in range(new_slots):
            present = taken > slot

            def kept(value):
                return jnp.where(present, value, jnp.zeros_like(value))

            if early(c):
                params[slot, rows(c)] = kept(wide_inbox[c][sources[slot]])
                outs[0][slot, rows(c)] = kept(wide_inbox[c][sources[slot], :, mine]).astype(jnp.float32)
            else:
                value = kept(inbox[c][sources[slot], 0])
                params[slot, rows(c), mine] = value
                outs[0][slot, rows(c)] = value.astype(jnp.float32)
            first = 0 if early(c) else 1
            for i in range(2):
                value = kept(inbox[c][sources[slot], first + i])
                outs[i + 1][slot, rows(c)] = value.astype(jnp.float32)
        if not early(c):
            gather(c)

    for c in range(min(AHEAD, chunks)):
        first_sends(c)
    zero = jnp.int32(0)
    _, taken, slots, sources = lax.fori_loop(
        0, tiles, route, (zero, zero, (zero,) * peers, (zero,) * new_slots)
    )
    slots = tuple(jnp.minimum(slot, stay.shape[0] - 1) for slot in slots)
    sources = tuple(jnp.minimum(source, owners - 1) for source in sources)
    jobs = []
    for c in range(chunks):
        if c >= AHEAD:
            jobs.append((c - AHEAD + 1, c, first_sends, (c,)))
        for at in range(1, dp - 1):
            jobs.append((c + at * HOP, c, relay, (c, at, True)))
            jobs.append((c + (dp - 1 - at) * HOP, c, relay, (c, at, False)))
        now = c + (dp - 1) * HOP
        jobs.append((now, c, update, (c,)))
        if not early(c):
            now += MAIL
            jobs.append((now, c, deliver, (c,)))
        for hop in range(1, dp - 1):
            jobs.append((now + hop * HOP, c, forward, (c, hop)))
        now += (dp - 1) * HOP
        if early(c):
            jobs.append((now, c, post_wide, (c,)))
            jobs.append((now + WIDE, c, deliver, (c,)))
        else:
            jobs.append((now, c, gathered, (c,)))
    for _, _, job, args in sorted(jobs, key=lambda item: item[:2]):
        job(*args)

    for c in range(chunks):
        for k in range(dp):
            reach = owns if early(c) else True

            @pl.when(reach & (z >= k) & (z < dp - 1))
            def _():
                gather_copy(c, k, True).wait_send()

            @pl.when(reach & (z <= k) & (z > 0))
            def _():
                gather_copy(c, k, False).wait_send()

        @pl.when(owns)
        def _():
            for k in range(1, dp):
                @pl.when(z < k)
                def _():
                    up_copy(c, k, False).wait_send()
            for k in range(dp - 1):
                @pl.when(z > k)
                def _():
                    down_copy(c, k, False).wait_send()
            for to in targets[1:]:
                mail_copy(c, to, e).wait_send()
                if early(c):
                    wide_copy(c, to, e).wait_send()


def shards(grad_parts, first_moment, second_moment, master_weight, old_owner, new_owner):
    dp = lax.axis_size("dp")
    peers = lax.axis_size("expert")
    old_slots, tile_rows, cols = first_moment.shape
    owners = old_owner.shape[0] // old_slots
    new_slots = min(old_slots + old_slots // 2, peers - peers // 5)
    chunks = tile_rows // ROWS
    bf16, f32 = jnp.bfloat16, jnp.float32
    dma = pltpu.SemaphoreType.DMA
    any_space = pl.BlockSpec(memory_space=pl.ANY)
    smem = pl.BlockSpec(memory_space=pltpu.SMEM)
    master = jax.ShapeDtypeStruct((new_slots, tile_rows, cols), f32)
    scratch = [
        pltpu.VMEM((old_slots, tile_rows, dp * cols), bf16),
        pltpu.VMEM((3, old_slots, tile_rows, cols), f32),
        pltpu.VMEM((dp, old_slots, tile_rows, cols), bf16),
        pltpu.VMEM((dp, old_slots, tile_rows, cols), bf16),
        pltpu.VMEM((dp, old_slots, tile_rows, cols), bf16),
        pltpu.VMEM((old_slots, ROWS, cols), f32),
    ]
    first = [early(c) for c in range(chunks)]
    kept = [2 if flag else 3 for flag in first]
    width = [dp * cols if flag else 128 for flag in first]
    span = [ROWS if flag else 16 for flag in first]
    scratch += [pltpu.VMEM((old_slots, n, ROWS, cols), bf16) for n in kept]
    scratch += [pltpu.VMEM((peers, n, ROWS, cols), bf16) for n in kept]
    scratch += [pltpu.VMEM((owners, n, ROWS, cols), bf16) for n in kept]
    scratch += [pltpu.VMEM((old_slots, r, n), bf16) for r, n in zip(span, width)]
    scratch += [pltpu.VMEM((peers, r, n), bf16) for r, n in zip(span, width)]
    scratch += [pltpu.VMEM((owners, r, n), bf16) for r, n in zip(span, width)]
    scratch += [dma((4,))] + [dma((chunks, dp))] * 4 + [dma((chunks, peers))] * 4
    scratch += [dma((chunks, dp))] * 4
    results = new_slots * tile_rows * cols * (12 + 2 * dp)
    return pl.pallas_call(
        functools.partial(kernel, dp, peers, owners, chunks),
        out_shape=(master,) * 3
        + (jax.ShapeDtypeStruct((new_slots, tile_rows, dp * cols), bf16),),
        in_specs=[smem] * 2 + [any_space] * 4,
        out_specs=(pl.BlockSpec(memory_space=pltpu.VMEM),) * 4,
        scratch_shapes=scratch,
        compiler_params=pltpu.CompilerParams(
            collective_id=0, has_side_effects=True, vmem_limit_bytes=67043328 - results - 2**19
        ),
    )(old_owner, new_owner, grad_parts, first_moment, second_moment, master_weight)


def solution(mesh):
    placed = (
        P("dp", "expert", None, None),
        P("expert", None, "dp"),
        P("expert", None, "dp"),
        P("expert", None, "dp"),
        P(),
        P(),
    )
    return jax.shard_map(
        shards,
        mesh=mesh,
        in_specs=placed,
        out_specs=(
            P("expert", None, "dp"),
            P("expert", None, "dp"),
            P("expert", None, "dp"),
            P("expert", None, None),
        ),
        check_vma=False,
    )
```

time: 111 us -> 96.4 us (0.87)
  Pallas kernels: 97.2 us -> 86.6 us
  other arithmetic: 4.21 us -> 0 us
    pallas_call x1, Pallas kernels: 97.2 us -> 86.6 us  [shards(): pl.pallas_call(functools.partial(kernel, dp, peers, owners, chunks), out_...]
    reduce_sum x3 -> x0, other arithmetic: 3.52 us -> none  [the longest x1 1.32 us: shards(): recv_has = jnp.sum(wanted.astype(jnp.int32), axis=1)]
where the time goes in v2:
time: 96.4 us; the launch traced here: 96.2 us
  Pallas kernels  86.6 us (90%)
  local copies, waits for them, and re-layouts  8.98 us (9%)
    pallas_call x1, Pallas kernels, shards(): pl.pallas_call(functools.partial(kernel, dp, peers, owners, chunks), out_...  86.6 us
    unnamed x10, local copies, waits for them, and re-layouts  8.98 us

profile of v2, /device:TPU:0, one launch (start us, length us, event | category | flops | bytes accessed | tf_op | source)
XLA Modules:
  0.0 96.2 jit_solution(13051052983296230431)
XLA Ops:
  0.6 86.6 %shard_map.93 = (f32[6,128,512]{2,1,0:T(8,128)}, f32[6,128,512]{2,1,0:T(8,128)}, f32[6,128,512]{2,1,0:T(8,128)}, bf16[6,128,2048]{2,1,0:T(8,128)(2,1)}) custom-call(s32[28]{0:T(128)} %old_ref.1, s32[28]{0:T(128)} %new_ref.1, bf16[1,4,128,2048]{3,2,1,0:T(8,128)(2,1)} %g_hbm.1, f32[4,128,512]{2,1,0:T(8,128)} %m_hbm.1, f32[4,128,512]{2,1,0:T(8,128)} %v_hbm.1, ...), custom_call_target="tpu_custom_call" | custom-call | tf_op jit(solution)/shard_map/pallas_call | solution.py:342
  87.3 0.0 copy-start.2
  87.3 2.9 %copy.14 = f32[6,128,512]{2,1,0:T(8,128)} copy(f32[6,128,512]{2,1,0:T(8,128)} %get-tuple-element.8) | data formatting | bytes 3145728
  90.1 0.0 copy-done.2
  90.1 0.0 copy-start.1
  90.1 1.1 %copy.15 = f32[6,128,512]{2,1,0:T(8,128)} copy(f32[6,128,512]{2,1,0:T(8,128)S(1)} %copy-done.2) | data formatting | bytes 3145728
  91.3 0.8 copy-done.1
  92.1 0.0 copy-start
  92.1 1.1 %copy.16 = f32[6,128,512]{2,1,0:T(8,128)} copy(f32[6,128,512]{2,1,0:T(8,128)S(1)} %copy-done.1) | data formatting | bytes 3145728
  93.3 1.3 %copy-done = bf16[6,128,2048]{2,1,0:T(8,128)(2,1)S(1)} copy-done((bf16[6,128,2048]{2,1,0:T(8,128)(2,1)S(1)}, bf16[6,128,2048]{2,1,0:T(8,128)(2,1)}, u32[]{:S(2)}) %copy-start) | copy-done | bytes 3145752
  94.6 1.7 %copy.17 = bf16[6,128,2048]{2,1,0:T(8,128)(2,1)} copy(bf16[6,128,2048]{2,1,0:T(8,128)(2,1)S(1)} %copy-done) | data formatting | bytes 6291456
Async XLA Ops:
  87.3 2.9 %copy-start.2 = (f32[6,128,512]{2,1,0:T(8,128)S(1)}, f32[6,128,512]{2,1,0:T(8,128)}, u32[]{:S(2)}) copy-start(f32[6,128,512]{2,1,0:T(8,128)} %get-tuple-element.9) | copy-start | bytes 4718596
  90.1 2.0 %copy-start.1 = (f32[6,128,512]{2,1,0:T(8,128)S(1)}, f32[6,128,512]{2,1,0:T(8,128)}, u32[]{:S(2)}) copy-start(f32[6,128,512]{2,1,0:T(8,128)} %get-tuple-element.10) | copy-start | bytes 4718596
  92.1 2.5 %copy-start = (bf16[6,128,2048]{2,1,0:T(8,128)(2,1)S(1)}, bf16[6,128,2048]{2,1,0:T(8,128)(2,1)}, u32[]{:S(2)}) copy-start(bf16[6,128,2048]{2,1,0:T(8,128)(2,1)} %get-tuple-element.11) | copy-start | bytes 9437188
